TPU v7x, 512 devices: a whole 4x4x16 slice. The times are simulated.
512 devices in a mesh: tm: 128 (over z, y, core), chan: 4 (over x).
Axes of the slice: x: 4, y: 4, z: 16, core: 2. Of those that a mesh axis runs over, the one named last changes fastest.
Arguments:
- markov: float32 [16384, 256, 4], P('tm', 'chan'), may hold values from -6 to 6
- sketch: float32 [16384, 4, 64], P('tm'), may hold values from -0.0234375 to 0.0234375
Outputs:
- basis: float32 [16384, 256, 64], P('tm', 'chan')
- factor: float32 [64, 64], replicated
All inputs are finite; a program needn't handle non-finite values.
Results may differ from a plain program's by a relative error of at most 0.000098.
Values sent between devices are 32-bit elements; how exact they have to be, the bound alone decides.
A program may use at most 128 MiB of HBM per device.

v0:
```python
import math
import jax
import jax.numpy as jnp
from jax import lax
from jax.sharding import PartitionSpec as P

HIGHEST_PREC = lax.Precision.HIGHEST


def circle(first, second, modulus):
    angle = (first[:, None] * second[None, :] % modulus).astype(jnp.float32) * (
        2.0 * math.pi / modulus
    )
    return (jnp.cos(angle), jnp.sin(angle))


def matmul_rows(matrix, blocks):
    return jnp.einsum("ab,bgw->agw", matrix, blocks, precision=HIGHEST_PREC)


def plain_dot(left, right):
    return jnp.dot(left, right, precision=HIGHEST_PREC)


def gram_of(matrix):
    return jnp.einsum("nr,ns->rs", matrix, matrix, precision=HIGHEST_PREC)


def product(left, right):
    return jnp.einsum("kpm,kmr->kpr", left, right, precision=HIGHEST_PREC)


def total_factor(gram_part, row_total):
    summed = lax.psum(gram_part, ("tm", "chan"))
    result = jnp.linalg.cholesky(summed / row_total)
    return result


def body(markov, sketch):
    seq_len = markov.shape[0]
    shards = lax.axis_size("tm")
    per_group = seq_len // shards
    whole_len = seq_len * shards
    own_index = lax.axis_index("tm")
    channels = markov.shape[1]
    inputs = markov.shape[2]
    columns = sketch.shape[2]
    row_total = whole_len * channels * lax.axis_size("chan")
    small_index = jnp.arange(shards, dtype=jnp.int32)
    time_index = jnp.arange(seq_len, dtype=jnp.int32)
    freq_index = own_index + shards * time_index
    cos_small, sin_small = circle(small_index, small_index, shards)
    cos_large, sin_large = circle(freq_index, time_index, whole_len)
    markov_blocks = markov.reshape(shards, per_group, channels * inputs)
    sketch_blocks = sketch.reshape(shards, per_group, inputs * columns)
    pieces = (
        lax.all_to_all(markov_blocks, "tm", split_axis=0, concat_axis=0, tiled=True),
        lax.all_to_all(sketch_blocks, "tm", split_axis=0, concat_axis=0, tiled=True),
    )
    results = []
    for piece_block in pieces:
        results.append(matmul_rows(cos_small, piece_block))
        results.append(-matmul_rows(sin_small, piece_block))
    spread = tuple(results)
    pieces = (
        lax.all_to_all(spread[0], "tm", split_axis=0, concat_axis=1, tiled=True),
        lax.all_to_all(spread[1], "tm", split_axis=0, concat_axis=1, tiled=True),
        lax.all_to_all(spread[2], "tm", split_axis=0, concat_axis=1, tiled=True),
        lax.all_to_all(spread[3], "tm", split_axis=0, concat_axis=1, tiled=True),
    )
    results = []
    for place in range(0, len(pieces), 2):
        real_part = pieces[place].reshape(seq_len, -1)
        imag_part = pieces[place + 1].reshape(seq_len, -1)
        results.append(plain_dot(cos_large, real_part) + plain_dot(sin_large, imag_part))
        results.append(plain_dot(cos_large, imag_part) - plain_dot(sin_large, real_part))
    markov_re, markov_im, sketch_re, sketch_im = tuple(results)
    markov_re = markov_re.reshape(seq_len, channels, inputs)
    markov_im = markov_im.reshape(seq_len, channels, inputs)
    sketch_re = sketch_re.reshape(seq_len, inputs, columns)
    sketch_im = sketch_im.reshape(seq_len, inputs, columns)
    spec_re = (product(markov_re, sketch_re) + product(markov_im, sketch_im)).reshape(
        seq_len * channels, columns
    )
    spec_im = (product(markov_im, sketch_re) - product(markov_re, sketch_im)).reshape(
        seq_len * channels, columns
    )
    identity_m = jnp.eye(columns, dtype=jnp.float32)
    real_part = spec_re.reshape(seq_len, channels * columns)
    imag_part = spec_im.reshape(seq_len, channels * columns)
    width = real_part.shape[1]
    turned_re = plain_dot(cos_large.T, real_part) - plain_dot(sin_large.T, imag_part)
    turned_im = plain_dot(sin_large.T, real_part) + plain_dot(cos_large.T, imag_part)
    pieces = (
        lax.all_to_all(
            turned_re.reshape(shards, per_group, width),
            "tm",
            split_axis=0,
            concat_axis=0,
            tiled=True,
        ),
        lax.all_to_all(
            turned_im.reshape(shards, per_group, width),
            "tm",
            split_axis=0,
            concat_axis=0,
            tiled=True,
        ),
    )
    mixed = (matmul_rows(cos_small, pieces[0]) - matmul_rows(sin_small, pieces[1])) / whole_len
    returned = lax.all_to_all(mixed, "tm", split_axis=0, concat_axis=1, tiled=True)
    result_time = returned.reshape(seq_len, width)
    signal = result_time
    signal = signal.reshape(seq_len * channels, columns)
    gram_part = gram_of(signal)
    lower_factor = total_factor(gram_part, row_total)
    inverse_t = jax.scipy.linalg.solve_triangular(lower_factor, identity_m, lower=True).T
    result = plain_dot(signal, inverse_t)
    return (result.reshape(seq_len, channels, columns), lower_factor.T)


def solution(mesh):
    return jax.shard_map(
        body,
        mesh=mesh,
        in_specs=(P("tm", "chan", None), P("tm", None, None)),
        out_specs=(P("tm", "chan", None), P()),
        check_vma=False,
    )
```

profile of v0, /device:TPU:1, one launch (start us, length us, event | category | flops | bytes accessed | tf_op | source)
XLA Modules:
  0.0 682.6 jit_solution(10656477915658200802)
XLA Ops:
  2.3 20.6 %all-to-all-start = ((f32[128,1,256]{2,1,0:T(1,128)}), f32[128,1,256]{2,1,0:T(1,128)S(1)}, u32[]{:S(2)}, u32[]{:S(2)}) async-start(f32[128,1,256]{2,1,0:T(1,128)} %copy.57), calls=%async_computation | async-start | bytes 262144 | tf_op jit(solution)/shard_map/all_to_all | solution.py:57
  24.5 14.3 %all-to-all-done = f32[128,1,256]{2,1,0:T(1,128)S(1)} async-done(((f32[128,1,256]{2,1,0:T(1,128)}), f32[128,1,256]{2,1,0:T(1,128)S(1)}, u32[]{:S(2)}, u32[]{:S(2)}) %all-to-all-start) | async-done | bytes 131104 | tf_op jit(solution)/shard_map/all_to_all | solution.py:57
  38.8 7.2 %all-to-all-start.3 = ((f32[128,1,256]{2,1,0:T(1,128)}), f32[128,1,256]{2,1,0:T(1,128)S(1)}, u32[]{:S(2)}, u32[]{:S(2)}) async-start(f32[128,1,256]{2,1,0:T(1,128)} %copy.61), calls=%async_computation.3 | async-start | bytes 262144 | tf_op jit(solution)/shard_map/all_to_all | solution.py:58
  47.4 14.6 %all-to-all-done.3 = f32[128,1,256]{2,1,0:T(1,128)S(1)} async-done(((f32[128,1,256]{2,1,0:T(1,128)}), f32[128,1,256]{2,1,0:T(1,128)S(1)}, u32[]{:S(2)}, u32[]{:S(2)}) %all-to-all-start.3) | async-done | bytes 131104 | tf_op jit(solution)/shard_map/all_to_all | solution.py:58
  62.0 7.3 %all-to-all-start.2 = ((f32[128,1,256]{2,1,0:T(1,128)}), f32[128,1,256]{2,1,0:T(1,128)S(1)}, u32[]{:S(2)}, u32[]{:S(2)}) async-start(f32[128,1,256]{2,1,0:T(1,128)} %copy.59), calls=%async_computation.2 | async-start | bytes 262144 | tf_op jit(solution)/shard_map/all_to_all | solution.py:67
  70.6 14.7 %all-to-all-done.2 = f32[128,1,256]{2,1,0:T(1,128)S(1)} async-done(((f32[128,1,256]{2,1,0:T(1,128)}), f32[128,1,256]{2,1,0:T(1,128)S(1)}, u32[]{:S(2)}, u32[]{:S(2)}) %all-to-all-start.2) | async-done | bytes 131104 | tf_op jit(solution)/shard_map/all_to_all | solution.py:67
  85.2 7.2 %all-to-all-start.1 = ((f32[128,1,256]{2,1,0:T(1,128)}), f32[128,1,256]{2,1,0:T(1,128)S(1)}, u32[]{:S(2)}, u32[]{:S(2)}) async-start(f32[128,1,256]{2,1,0:T(1,128)} %copy.58), calls=%async_computation.1 | async-start | bytes 262144 | tf_op jit(solution)/shard_map/all_to_all | solution.py:66
  93.8 14.7 %all-to-all-done.1 = f32[128,1,256]{2,1,0:T(1,128)S(1)} async-done(((f32[128,1,256]{2,1,0:T(1,128)}), f32[128,1,256]{2,1,0:T(1,128)S(1)}, u32[]{:S(2)}, u32[]{:S(2)}) %all-to-all-start.1) | async-done | bytes 131104 | tf_op jit(solution)/shard_map/all_to_all | solution.py:66
  108.5 7.7 %all-to-all-start.5 = ((f32[128,1,256]{2,1,0:T(1,128)}), f32[128,1,256]{2,1,0:T(1,128)S(1)}, u32[]{:S(2)}, u32[]{:S(2)}) async-start(f32[128,1,256]{2,1,0:T(1,128)} %copy.63), calls=%async_computation.5 | async-start | bytes 262144 | tf_op jit(solution)/shard_map/all_to_all | solution.py:69
  118.6 13.5 %all-to-all-done.5 = f32[128,1,256]{2,1,0:T(1,128)S(1)} async-done(((f32[128,1,256]{2,1,0:T(1,128)}), f32[128,1,256]{2,1,0:T(1,128)S(1)}, u32[]{:S(2)}, u32[]{:S(2)}) %all-to-all-start.5) | async-done | bytes 131104 | tf_op jit(solution)/shard_map/all_to_all | solution.py:69
  132.1 7.2 %all-to-all-start.4 = ((f32[128,1,256]{2,1,0:T(1,128)}), f32[128,1,256]{2,1,0:T(1,128)S(1)}, u32[]{:S(2)}, u32[]{:S(2)}) async-start(f32[128,1,256]{2,1,0:T(1,128)} %copy.62), calls=%async_computation.4 | async-start | bytes 262144 | tf_op jit(solution)/shard_map/all_to_all | solution.py:68
  141.4 13.8 %all-to-all-done.4 = f32[128,1,256]{2,1,0:T(1,128)S(1)} async-done(((f32[128,1,256]{2,1,0:T(1,128)}), f32[128,1,256]{2,1,0:T(1,128)S(1)}, u32[]{:S(2)}, u32[]{:S(2)}) %all-to-all-start.4) | async-done | bytes 131104 | tf_op jit(solution)/shard_map/all_to_all | solution.py:68
  157.4 6.7 fusion.151
  164.1 8.4 %fusion.150 = f32[128,64,64]{2,1,0:T(8,128)} fusion(f32[128,64,4]{1,2,0:T(4,128)S(1)} %copy.65, f32[128,4,64]{2,1,0:T(4,128)S(1)} %copy.66), kind=kOutput, calls=%fused_computation.161 | convolution fusion | flops 25165824 | bytes 2359296 | tf_op jit(solution)/shard_map/kpm,kmr->kpr/dot_general | solution.py:30
  172.5 8.3 %convolution_subtract_fusion.2 = f32[128,64,64]{2,1,0:T(8,128)} fusion(f32[128,64,64]{2,1,0:T(8,128)S(1)} %fusion.151, f32[128,64,4]{1,2,0:T(4,128)S(1)} %copy.65, f32[128,4,64]{2,1,0:T(4,128)S(1)} %copy.70), kind=kOutput, calls=%fused_computation.7 | convolution fusion | flops 25690112 | bytes 4456448 | tf_op jit(solution)/shard_map/kpm,kmr->kpr/dot_general | solution.py:30
  184.6 9.8 %convolution_add_fusion.1 = f32[128,64,64]{2,1,0:T(8,128)} fusion(f32[128,64,64]{2,1,0:T(8,128)} %fusion.150, f32[128,64,4]{1,2,0:T(4,128)S(1)} %copy.69, f32[128,4,64]{2,1,0:T(4,128)S(1)} %copy.70), kind=kOutput, calls=%fused_computation.8 | convolution fusion | flops 25690112 | bytes 4456448 | tf_op jit(solution)/shard_map/kpm,kmr->kpr/dot_general | solution.py:30
  194.4 4.9 copy.71
  209.0 8.3 %all-to-all-start.6 = ((f32[128,1,4096]{2,1,0:T(1,128)}), f32[128,1,4096]{2,1,0:T(1,128)}, u32[]{:S(2)}, u32[]{:S(2)}) async-start(f32[128,1,4096]{2,1,0:T(1,128)} %copy.77), calls=%async_computation.6 | async-start | bytes 4194304 | tf_op jit(solution)/shard_map/all_to_all | solution.py:95
  226.8 85.7 %all-to-all-done.6 = f32[128,1,4096]{2,1,0:T(1,128)} async-done(((f32[128,1,4096]{2,1,0:T(1,128)}), f32[128,1,4096]{2,1,0:T(1,128)}, u32[]{:S(2)}, u32[]{:S(2)}) %all-to-all-start.6) | async-done | bytes 2097184 | tf_op jit(solution)/shard_map/all_to_all | solution.py:95
  312.6 11.3 %all-to-all-start.7 = ((f32[128,1,4096]{2,1,0:T(1,128)}), f32[128,1,4096]{2,1,0:T(1,128)S(1)}, u32[]{:S(2)}, u32[]{:S(2)}) async-start(f32[128,1,4096]{2,1,0:T(1,128)} %copy.78), calls=%async_computation.7 | async-start | bytes 4194304 | tf_op jit(solution)/shard_map/all_to_all | solution.py:102
  323.9 6.0 fusion.6
  329.9 89.8 %all-to-all-done.7 = f32[128,1,4096]{2,1,0:T(1,128)S(1)} async-done(((f32[128,1,4096]{2,1,0:T(1,128)}), f32[128,1,4096]{2,1,0:T(1,128)S(1)}, u32[]{:S(2)}, u32[]{:S(2)}) %all-to-all-start.7) | async-done | bytes 2097184 | tf_op jit(solution)/shard_map/all_to_all | solution.py:102
  419.7 4.9 fusion.1
  426.7 107.0 %all_to_all.65 = f32[128,1,4096]{2,1,0:T(1,128)S(1)} all-to-all(f32[128,1,4096]{2,1,0:T(1,128)S(1)} %copy.79), channel_id=1, replica_groups=mesh['tm'=128,'chan'=4] {'tm'}, dimensions={0} | all-to-all | bytes 4194304 | tf_op jit(solution)/shard_map/all_to_all | solution.py:111
  533.7 7.3 %reduce.6 = f32[128,4096]{1,0:T(8,128)} reduce(f32[128,1,4096]{2,1,0:T(1,128)S(1)} %all_to_all.65, f32[]{:T(128)} %constant.86), dimensions={1}, to_apply=%all_to_all.26.reduce_sub_computation | reduce | bytes 4194308 | tf_op jit(solution)/shard_map/all_to_all | solution.py:111
  541.0 4.8 reshape_reshape.11
  545.8 10.4 %fusion.152 = f32[64,64]{0,1:T(8,128)S(1)} fusion(f32[8192,64]{1,0:T(8,128)} %reshape_reshape.11), kind=kOutput, calls=%fused_computation.163 | convolution fusion | flops 402653184 | bytes 2113536 | tf_op jit(solution)/shard_map/nr,ns->rs/dot_general | solution.py:26
  556.2 104.1 %psum.7 = f32[64,64]{0,1:T(8,128)S(1)} all-reduce(f32[64,64]{0,1:T(8,128)S(1)} %fusion.152), channel_id=1, replica_groups=mesh['tm'=128,'chan'=4] {'tm','chan'}, use_global_device_ids=true, to_apply=%region_0.1 | all-reduce | flops 4096 | bytes 32768 | tf_op jit(solution)/shard_map/psum | solution.py:34
  660.5 5.8 cholesky.17
  668.3 4.9 custom-call.7
  673.5 3.8 copy.80
  677.3 4.9 fusion.153
  (43 shorter events, 41.4 us)
Async XLA Ops:
  2.3 36.6 %all-to-all-start = ((f32[128,1,256]{2,1,0:T(1,128)}), f32[128,1,256]{2,1,0:T(1,128)S(1)}, u32[]{:S(2)}, u32[]{:S(2)}) async-start(f32[128,1,256]{2,1,0:T(1,128)} %copy.57), calls=%async_computation | async-start | bytes 262144 | tf_op jit(solution)/shard_map/all_to_all | solution.py:57
  38.8 23.2 %all-to-all-start.3 = ((f32[128,1,256]{2,1,0:T(1,128)}), f32[128,1,256]{2,1,0:T(1,128)S(1)}, u32[]{:S(2)}, u32[]{:S(2)}) async-start(f32[128,1,256]{2,1,0:T(1,128)} %copy.61), calls=%async_computation.3 | async-start | bytes 262144 | tf_op jit(solution)/shard_map/all_to_all | solution.py:58
  62.0 23.3 %all-to-all-start.2 = ((f32[128,1,256]{2,1,0:T(1,128)}), f32[128,1,256]{2,1,0:T(1,128)S(1)}, u32[]{:S(2)}, u32[]{:S(2)}) async-start(f32[128,1,256]{2,1,0:T(1,128)} %copy.59), calls=%async_computation.2 | async-start | bytes 262144 | tf_op jit(solution)/shard_map/all_to_all | solution.py:67
  85.2 23.2 %all-to-all-start.1 = ((f32[128,1,256]{2,1,0:T(1,128)}), f32[128,1,256]{2,1,0:T(1,128)S(1)}, u32[]{:S(2)}, u32[]{:S(2)}) async-start(f32[128,1,256]{2,1,0:T(1,128)} %copy.58), calls=%async_computation.1 | async-start | bytes 262144 | tf_op jit(solution)/shard_map/all_to_all | solution.py:66
  108.5 23.6 %all-to-all-start.5 = ((f32[128,1,256]{2,1,0:T(1,128)}), f32[128,1,256]{2,1,0:T(1,128)S(1)}, u32[]{:S(2)}, u32[]{:S(2)}) async-start(f32[128,1,256]{2,1,0:T(1,128)} %copy.63), calls=%async_computation.5 | async-start | bytes 262144 | tf_op jit(solution)/shard_map/all_to_all | solution.py:69
  132.1 23.1 %all-to-all-start.4 = ((f32[128,1,256]{2,1,0:T(1,128)}), f32[128,1,256]{2,1,0:T(1,128)S(1)}, u32[]{:S(2)}, u32[]{:S(2)}) async-start(f32[128,1,256]{2,1,0:T(1,128)} %copy.62), calls=%async_computation.4 | async-start | bytes 262144 | tf_op jit(solution)/shard_map/all_to_all | solution.py:68
  209.0 103.6 %all-to-all-start.6 = ((f32[128,1,4096]{2,1,0:T(1,128)}), f32[128,1,4096]{2,1,0:T(1,128)}, u32[]{:S(2)}, u32[]{:S(2)}) async-start(f32[128,1,4096]{2,1,0:T(1,128)} %copy.77), calls=%async_computation.6 | async-start | bytes 4194304 | tf_op jit(solution)/shard_map/all_to_all | solution.py:95
  312.6 107.1 %all-to-all-start.7 = ((f32[128,1,4096]{2,1,0:T(1,128)}), f32[128,1,4096]{2,1,0:T(1,128)S(1)}, u32[]{:S(2)}, u32[]{:S(2)}) async-start(f32[128,1,4096]{2,1,0:T(1,128)} %copy.78), calls=%async_computation.7 | async-start | bytes 4194304 | tf_op jit(solution)/shard_map/all_to_all | solution.py:102
where the time goes:
time: 692 us; the launch traced here: 683 us
  waiting for transfers between devices  261 us (38%)
  blocking collectives  211 us (30%)
  matrix products  78.4 us (11%)
  starting transfers between devices  76.6 us (11%)
  local copies, waits for them, and re-layouts  34.7 us (5%)
  other arithmetic  19.3 us (3%)
    all_to_all x1, blocking collectives, body(): lax.all_to_all(mixed, 'tm', split_axis=0, concat_axis=1, tiled=True)  107 us
    psum x1, blocking collectives, total_factor(): summed = lax.psum(gram_part, ('tm', 'chan'))  104 us
    all_to_all x1, waiting for transfers between devices, body(): lax.all_to_all(turned_im.reshape(shards, per_group, width), 'tm', split_a...  89.8 us
    all_to_all x1, waiting for transfers between devices, body(): lax.all_to_all(turned_re.reshape(shards, per_group, width), 'tm', split_a...  85.7 us
    dot_general x4, matrix products, product(): return jnp.einsum('kpm,kmr->kpr', left, right, precision=HIGHEST_PREC)  33.2 us
    dot_general x13, matrix products, plain_dot(): return jnp.dot(left, right, precision=HIGHEST_PREC)  21.6 us
    all_to_all x1, starting transfers between devices, body(): lax.all_to_all(markov_blocks, 'tm', split_axis=0, concat_axis=0, tiled=True)  20.6 us
    all_to_all x1, waiting for transfers between devices, body(): lax.all_to_all(spread[1], 'tm', split_axis=0, concat_axis=1, tiled=True)  14.7 us
  transfers between devices with their start and end apart: 8, of which 8 were waited for; matrix products, arithmetic and copies ran while one was open for 4% of the time, Pallas kernels for 0%

commit v1 on v0

--- a/solution.py
+++ b/solution.py
@@ -31,7 +31,7 @@
 
 
 def total_factor(gram_part, row_total):
-    summed = lax.psum(gram_part, ("tm", "chan"))
+    summed = jnp.sum(lax.all_gather(gram_part, ("tm", "chan")), axis=0)
     result = jnp.linalg.cholesky(summed / row_total)
     return result
 

time: 692 us -> 819 us (1.18)
  waiting for transfers between devices: 261 us -> 473 us
  blocking collectives: 211 us -> 107 us
  between operations: 1.41 us -> 14.9 us
    all_gather x0 -> x1, waiting for transfers between devices: none -> 212 us  [total_factor(): summed = jnp.sum(lax.all_gather(gram_part, ('tm', 'chan')), axis=0)]
    psum x1 -> x0, blocking collectives: 104 us -> none  [total_factor(): summed = lax.psum(gram_part, ('tm', 'chan'))]
  transfers between devices with their start and end apart: 8 -> 9, of which waited for: 8 -> 9; matrix products, arithmetic and copies ran while one was open for 4% -> 4% of each run, Pallas kernels for 0% -> 0%
where the time goes in v1:
time: 819 us; the launch traced here: 810 us
  waiting for transfers between devices  473 us (58%)
  blocking collectives  107 us (13%)
  matrix products  77.5 us (9%)
  starting transfers between devices  76.5 us (9%)
  local copies, waits for them, and re-layouts  35 us (4%)
  other arithmetic  26.4 us (3%)
  between operations  14.9 us (2%)
    all_gather x1, waiting for transfers between devices, total_factor(): summed = jnp.sum(lax.all_gather(gram_part, ('tm', 'chan')), axis=0)  212 us
    all_to_all x1, blocking collectives, body(): lax.all_to_all(mixed, 'tm', split_axis=0, concat_axis=1, tiled=True)  107 us
    all_to_all x1, waiting for transfers between devices, body(): lax.all_to_all(turned_im.reshape(shards, per_group, width), 'tm', split_a...  89.7 us
    all_to_all x1, waiting for transfers between devices, body(): lax.all_to_all(turned_re.reshape(shards, per_group, width), 'tm', split_a...  85.8 us
    dot_general x4, matrix products, product(): return jnp.einsum('kpm,kmr->kpr', left, right, precision=HIGHEST_PREC)  33.2 us
    all_to_all x1, starting transfers between devices, body(): lax.all_to_all(markov_blocks, 'tm', split_axis=0, concat_axis=0, tiled=True)  20.6 us
    dot_general x13, matrix products, plain_dot(): return jnp.dot(left, right, precision=HIGHEST_PREC)  20.1 us
  transfers between devices with their start and end apart: 9, of which 9 were waited for; matrix products, arithmetic and copies ran while one was open for 4% of the time, Pallas kernels for 0%

profile of v1, /device:TPU:1, one launch (start us, length us, event | category | flops | bytes accessed | tf_op | source)
XLA Modules:
  0.0 810.3 jit_solution(5839791852053315633)
XLA Ops:
  8.8 20.6 %all-to-all-start = ((f32[128,1,256]{2,1,0:T(1,128)}), f32[128,1,256]{2,1,0:T(1,128)S(1)}, u32[]{:S(2)}, u32[]{:S(2)}) async-start(f32[128,1,256]{2,1,0:T(1,128)} %copy.54), calls=%async_computation | async-start | bytes 262144 | tf_op jit(solution)/shard_map/all_to_all | solution.py:57
  31.0 14.3 %all-to-all-done = f32[128,1,256]{2,1,0:T(1,128)S(1)} async-done(((f32[128,1,256]{2,1,0:T(1,128)}), f32[128,1,256]{2,1,0:T(1,128)S(1)}, u32[]{:S(2)}, u32[]{:S(2)}) %all-to-all-start) | async-done | bytes 131104 | tf_op jit(solution)/shard_map/all_to_all | solution.py:57
  45.4 7.2 all-to-all-start.3
  53.9 14.7 %all-to-all-done.3 = f32[128,1,256]{2,1,0:T(1,128)S(1)} async-done(((f32[128,1,256]{2,1,0:T(1,128)}), f32[128,1,256]{2,1,0:T(1,128)S(1)}, u32[]{:S(2)}, u32[]{:S(2)}) %all-to-all-start.3) | async-done | bytes 131104 | tf_op jit(solution)/shard_map/all_to_all | solution.py:58
  68.6 7.2 all-to-all-start.2
  77.1 14.7 %all-to-all-done.2 = f32[128,1,256]{2,1,0:T(1,128)S(1)} async-done(((f32[128,1,256]{2,1,0:T(1,128)}), f32[128,1,256]{2,1,0:T(1,128)S(1)}, u32[]{:S(2)}, u32[]{:S(2)}) %all-to-all-start.2) | async-done | bytes 131104 | tf_op jit(solution)/shard_map/all_to_all | solution.py:67
  91.8 7.2 all-to-all-start.1
  100.3 14.7 %all-to-all-done.1 = f32[128,1,256]{2,1,0:T(1,128)S(1)} async-done(((f32[128,1,256]{2,1,0:T(1,128)}), f32[128,1,256]{2,1,0:T(1,128)S(1)}, u32[]{:S(2)}, u32[]{:S(2)}) %all-to-all-start.1) | async-done | bytes 131104 | tf_op jit(solution)/shard_map/all_to_all | solution.py:66
  115.0 7.7 all-to-all-start.5
  125.1 13.5 %all-to-all-done.5 = f32[128,1,256]{2,1,0:T(1,128)S(1)} async-done(((f32[128,1,256]{2,1,0:T(1,128)}), f32[128,1,256]{2,1,0:T(1,128)S(1)}, u32[]{:S(2)}, u32[]{:S(2)}) %all-to-all-start.5) | async-done | bytes 131104 | tf_op jit(solution)/shard_map/all_to_all | solution.py:69
  138.6 7.2 all-to-all-start.4
  148.0 13.8 %all-to-all-done.4 = f32[128,1,256]{2,1,0:T(1,128)S(1)} async-done(((f32[128,1,256]{2,1,0:T(1,128)}), f32[128,1,256]{2,1,0:T(1,128)S(1)}, u32[]{:S(2)}, u32[]{:S(2)}) %all-to-all-start.4) | async-done | bytes 131104 | tf_op jit(solution)/shard_map/all_to_all | solution.py:68
  164.0 6.7 fusion.151
  170.7 8.4 %fusion.150 = f32[128,64,64]{2,1,0:T(8,128)} fusion(f32[128,64,4]{1,2,0:T(4,128)S(1)} %copy.62, f32[128,4,64]{2,1,0:T(4,128)S(1)} %copy.63), kind=kOutput, calls=%fused_computation.160 | convolution fusion | flops 25165824 | bytes 2359296 | tf_op jit(solution)/shard_map/kpm,kmr->kpr/dot_general | solution.py:30
  179.1 8.3 %convolution_subtract_fusion.2 = f32[128,64,64]{2,1,0:T(8,128)} fusion(f32[128,64,64]{2,1,0:T(8,128)S(1)} %fusion.151, f32[128,64,4]{1,2,0:T(4,128)S(1)} %copy.62, f32[128,4,64]{2,1,0:T(4,128)S(1)} %copy.67), kind=kOutput, calls=%fused_computation.7 | convolution fusion | flops 25690112 | bytes 4456448 | tf_op jit(solution)/shard_map/kpm,kmr->kpr/dot_general | solution.py:30
  191.2 9.8 %convolution_add_fusion.1 = f32[128,64,64]{2,1,0:T(8,128)} fusion(f32[128,64,64]{2,1,0:T(8,128)} %fusion.150, f32[128,64,4]{1,2,0:T(4,128)S(1)} %copy.66, f32[128,4,64]{2,1,0:T(4,128)S(1)} %copy.67), kind=kOutput, calls=%fused_computation.8 | convolution fusion | flops 25690112 | bytes 4456448 | tf_op jit(solution)/shard_map/kpm,kmr->kpr/dot_general | solution.py:30
  201.0 4.9 copy.68
  215.5 8.2 %all-to-all-start.6 = ((f32[128,1,4096]{2,1,0:T(1,128)}), f32[128,1,4096]{2,1,0:T(1,128)}, u32[]{:S(2)}, u32[]{:S(2)}) async-start(f32[128,1,4096]{2,1,0:T(1,128)} %copy.74), calls=%async_computation.6 | async-start | bytes 4194304 | tf_op jit(solution)/shard_map/all_to_all | solution.py:95
  233.4 85.8 %all-to-all-done.6 = f32[128,1,4096]{2,1,0:T(1,128)} async-done(((f32[128,1,4096]{2,1,0:T(1,128)}), f32[128,1,4096]{2,1,0:T(1,128)}, u32[]{:S(2)}, u32[]{:S(2)}) %all-to-all-start.6) | async-done | bytes 2097184 | tf_op jit(solution)/shard_map/all_to_all | solution.py:95
  319.2 11.0 %all-to-all-start.7 = ((f32[128,1,4096]{2,1,0:T(1,128)}), f32[128,1,4096]{2,1,0:T(1,128)S(1)}, u32[]{:S(2)}, u32[]{:S(2)}) async-start(f32[128,1,4096]{2,1,0:T(1,128)} %copy.75), calls=%async_computation.7 | async-start | bytes 4194304 | tf_op jit(solution)/shard_map/all_to_all | solution.py:102
  330.4 6.0 fusion.6
  336.4 89.7 %all-to-all-done.7 = f32[128,1,4096]{2,1,0:T(1,128)S(1)} async-done(((f32[128,1,4096]{2,1,0:T(1,128)}), f32[128,1,4096]{2,1,0:T(1,128)S(1)}, u32[]{:S(2)}, u32[]{:S(2)}) %all-to-all-start.7) | async-done | bytes 2097184 | tf_op jit(solution)/shard_map/all_to_all | solution.py:102
  426.1 4.9 fusion.1
  433.2 107.0 %all_to_all.65 = f32[128,1,4096]{2,1,0:T(1,128)S(1)} all-to-all(f32[128,1,4096]{2,1,0:T(1,128)S(1)} %copy.76), channel_id=1, replica_groups=mesh['tm'=128,'chan'=4] {'tm'}, dimensions={0} | all-to-all | bytes 4194304 | tf_op jit(solution)/shard_map/all_to_all | solution.py:111
  540.1 7.3 reduce.6
  547.4 4.8 reshape_reshape.11
  552.2 11.1 %fusion.152 = f32[64,64]{1,0:T(8,128)} fusion(f32[8192,64]{1,0:T(8,128)} %reshape_reshape.11), kind=kOutput, calls=%fused_computation.162 | convolution fusion | flops 402653184 | bytes 2113536 | tf_op jit(solution)/shard_map/nr,ns->rs/dot_general | solution.py:26
  563.3 4.1 copy.77
  567.4 212.0 %all-gather.3.cloned.1.call-done = f32[32768,64]{1,0:T(8,128)} async-done(((f32[64,64]{1,0:T(8,128)}), f32[32768,64]{1,0:T(8,128)}) %all-gather.3.cloned.1.call-update) | async-done | bytes 8388624 | tf_op jit(solution)/shard_map/all_gather | solution.py:34
  779.5 7.1 reduce_sum.11
  786.6 5.8 cholesky.17
  794.5 4.9 custom-call.7
  (47 shorter events, 45.0 us)
Async XLA Ops:
  8.8 36.6 %all-to-all-start = ((f32[128,1,256]{2,1,0:T(1,128)}), f32[128,1,256]{2,1,0:T(1,128)S(1)}, u32[]{:S(2)}, u32[]{:S(2)}) async-start(f32[128,1,256]{2,1,0:T(1,128)} %copy.54), calls=%async_computation | async-start | bytes 262144 | tf_op jit(solution)/shard_map/all_to_all | solution.py:57
  45.4 23.2 %all-to-all-start.3 = ((f32[128,1,256]{2,1,0:T(1,128)}), f32[128,1,256]{2,1,0:T(1,128)S(1)}, u32[]{:S(2)}, u32[]{:S(2)}) async-start(f32[128,1,256]{2,1,0:T(1,128)} %copy.58), calls=%async_computation.3 | async-start | bytes 262144 | tf_op jit(solution)/shard_map/all_to_all | solution.py:58
  68.6 23.2 %all-to-all-start.2 = ((f32[128,1,256]{2,1,0:T(1,128)}), f32[128,1,256]{2,1,0:T(1,128)S(1)}, u32[]{:S(2)}, u32[]{:S(2)}) async-start(f32[128,1,256]{2,1,0:T(1,128)} %copy.56), calls=%async_computation.2 | async-start | bytes 262144 | tf_op jit(solution)/shard_map/all_to_all | solution.py:67
  91.8 23.2 %all-to-all-start.1 = ((f32[128,1,256]{2,1,0:T(1,128)}), f32[128,1,256]{2,1,0:T(1,128)S(1)}, u32[]{:S(2)}, u32[]{:S(2)}) async-start(f32[128,1,256]{2,1,0:T(1,128)} %copy.55), calls=%async_computation.1 | async-start | bytes 262144 | tf_op jit(solution)/shard_map/all_to_all | solution.py:66
  115.0 23.6 %all-to-all-start.5 = ((f32[128,1,256]{2,1,0:T(1,128)}), f32[128,1,256]{2,1,0:T(1,128)S(1)}, u32[]{:S(2)}, u32[]{:S(2)}) async-start(f32[128,1,256]{2,1,0:T(1,128)} %copy.60), calls=%async_computation.5 | async-start | bytes 262144 | tf_op jit(solution)/shard_map/all_to_all | solution.py:69
  138.6 23.2 %all-to-all-start.4 = ((f32[128,1,256]{2,1,0:T(1,128)}), f32[128,1,256]{2,1,0:T(1,128)S(1)}, u32[]{:S(2)}, u32[]{:S(2)}) async-start(f32[128,1,256]{2,1,0:T(1,128)} %copy.59), calls=%async_computation.4 | async-start | bytes 262144 | tf_op jit(solution)/shard_map/all_to_all | solution.py:68
  215.5 103.6 %all-to-all-start.6 = ((f32[128,1,4096]{2,1,0:T(1,128)}), f32[128,1,4096]{2,1,0:T(1,128)}, u32[]{:S(2)}, u32[]{:S(2)}) async-start(f32[128,1,4096]{2,1,0:T(1,128)} %copy.74), calls=%async_computation.6 | async-start | bytes 4194304 | tf_op jit(solution)/shard_map/all_to_all | solution.py:95
  319.2 107.0 %all-to-all-start.7 = ((f32[128,1,4096]{2,1,0:T(1,128)}), f32[128,1,4096]{2,1,0:T(1,128)S(1)}, u32[]{:S(2)}, u32[]{:S(2)}) async-start(f32[128,1,4096]{2,1,0:T(1,128)} %copy.75), calls=%async_computation.7 | async-start | bytes 4194304 | tf_op jit(solution)/shard_map/all_to_all | solution.py:102
  330.2 449.2 %all-gather.3.cloned.1.call-start = ((), (), s32[]{:S(2)}) async-start(), calls=%async_computation.9 | async-start | bytes 16809984 | tf_op jit(solution)/shard_map/all_gather | solution.py:34
  779.5 20.2 %copy-start = (f32[128,1,4096]{0,2,1:T(8,128)S(1)}, f32[128,1,4096]{0,2,1:T(8,128)}, u32[]{:S(2)}) copy-start(f32[128,1,4096]{0,2,1:T(8,128)} %copy.77) | copy-start | bytes 6291460
Sparse Core Ops, SparseCore 0:
  563.5 215.9 all-gather.2
